TPU v7x, 32 devices: a whole 2x2x4 slice. The times are simulated.
32 devices in a mesh: dp: 2 (over core), expert: 16 (over z, y, x).
Axes of the slice: x: 2, y: 2, z: 4, core: 2. Of those that a mesh axis runs over, the one named last changes fastest.
Arguments:
- residual: bfloat16 [2048, 4096], P(('dp', 'expert')), may hold values from -6 to 6
- attn_out: bfloat16 [2048, 4096], P(('dp', 'expert')), may hold values from -6 to 6
- norm_gain: float32 [4096], replicated, may hold values from 0.5 to 2
- routes: int32 [2048, 8], P(('dp', 'expert')), may hold values from 0 to 15, all different within a row; in each aligned block of 64 rows (0 to 63, 64 to 127, ...) at most 40 rows name the same one
- mixing: float32 [2048, 8], P(('dp', 'expert')), may hold values from 0.05 to 0.35
- gate_w: bfloat16 [16, 4096, 768], P('expert', None, 'dp'), may hold values from -0.09375 to 0.09375
- up_w: bfloat16 [16, 4096, 768], P('expert', None, 'dp'), may hold values from -0.09375 to 0.09375
- down_w: bfloat16 [16, 768, 4096], P('expert', 'dp'), may hold values from -0.21875 to 0.21875
Outputs:
- layer_out: bfloat16 [2048, 4096], P(('dp', 'expert'))
Inputs may be any that keep to these rules, and one draw needn't show every extreme that they name: `routes`: each row names 8 different experts; within the rows of one device (aligned blocks of 64 rows) no expert is named by more than 40 rows.
All inputs are finite; a program needn't handle non-finite values.
Results may differ from a plain program's by a relative error of at most 0.0041.
Values may be sent and summed in bfloat16 or wider, within the bound.
A program may use at most 128 MiB of HBM per device.

v0:
```python
import jax
import jax.numpy as jnp
from jax import lax
from jax.sharding import PartitionSpec as P


def run_expert(inputs, gate_part, up_part, down_part):
    width = inputs.shape[-1]
    flat_rows = inputs.reshape(-1, width)
    gate = jnp.dot(flat_rows, gate_part, preferred_element_type=jnp.float32)
    up = jnp.dot(flat_rows, up_part, preferred_element_type=jnp.float32)
    hidden = (jax.nn.silu(gate) * up).astype(jnp.bfloat16)
    result = jnp.dot(hidden, down_part, preferred_element_type=jnp.float32)
    return result.reshape(inputs.shape)


def shards(residual, attn_out, norm_gain, routes, mixing, gate_w, up_w, down_w):
    experts = lax.axis_size("expert")
    rows, top = routes.shape
    width = residual.shape[1]
    capacity = max(2, 5 * rows * top // (4 * experts))
    slots = experts * capacity
    stream = residual.astype(jnp.float32) + attn_out.astype(jnp.float32)
    square = jnp.mean(stream * stream, axis=1, keepdims=True)
    normed = (stream * lax.rsqrt(square + 1e-06) * norm_gain[None, :]).astype(jnp.bfloat16)
    flat_routes = routes.reshape(-1)
    onehot = (flat_routes[:, None] == jnp.arange(experts, dtype=jnp.int32)[None, :]).astype(
        jnp.int32
    )
    earlier = jnp.cumsum(onehot, axis=0) - onehot
    position = jnp.sum(earlier * onehot, axis=1)
    slot_of = flat_routes * capacity + position
    selector = slot_of[None, :] == jnp.arange(slots, dtype=jnp.int32)[:, None]
    selector = jnp.any(selector.reshape(slots, rows, top), axis=2).astype(jnp.bfloat16)
    packed = jnp.dot(selector, normed, preferred_element_type=jnp.float32).astype(jnp.bfloat16)
    packed = packed.reshape(experts, capacity, width)
    gate_full, up_full = (
        lax.all_gather(gate_w, "dp", axis=2, tiled=True),
        lax.all_gather(up_w, "dp", axis=2, tiled=True),
    )
    down_full = lax.all_gather(down_w, "dp", axis=1, tiled=True)
    returned = lax.all_to_all(
        run_expert(
            lax.all_to_all(packed, "expert", split_axis=0, concat_axis=0, tiled=True),
            gate_full[0],
            up_full[0],
            down_full[0],
        ).astype(jnp.bfloat16),
        "expert",
        split_axis=0,
        concat_axis=0,
        tiled=True,
    )
    returned = returned.reshape(slots, width)
    taken = returned[slot_of].reshape(rows, top, width)
    mixed = jnp.sum(taken.astype(jnp.float32) * mixing[:, :, None], axis=1)
    return (stream + mixed).astype(jnp.bfloat16)


def solution(mesh):
    return jax.shard_map(
        shards,
        mesh=mesh,
        in_specs=(
            P(("dp", "expert"), None),
            P(("dp", "expert"), None),
            P(),
            P(("dp", "expert"), None),
            P(("dp", "expert"), None),
            P("expert", None, "dp"),
            P("expert", None, "dp"),
            P("expert", "dp", None),
        ),
        out_specs=P(("dp", "expert"), None),
        check_vma=False,
    )
```

profile of v0, /device:TPU:14, one launch (start us, length us, event | category | flops | bytes accessed | tf_op | source)
XLA Modules:
  0.0 313.7 jit_solution(4998074516552940635)
XLA Ops:
  6.5 0.0 copy-start.3
  6.5 0.0 copy-start.1
  6.5 0.0 copy-start
  6.5 0.0 copy-start.2
  6.5 0.0 all-gather.4.cloned.1.call-start
  6.6 0.7 all-gather.4.cloned.1.call-update
  7.3 0.0 all-gather.6.cloned.1.call-start
  7.3 0.7 all-gather.6.cloned.1.call-update
  8.0 0.0 copy-done.3
  8.0 0.1 copy.16
  8.1 0.1 eq.43
  8.2 0.1 eq.39
  8.3 1.2 reduce-window.6
  9.5 0.2 slice_reduce_fusion
  9.7 0.1 fusion.13
  9.8 0.1 reduce_sum.32
  9.9 0.5 fusion.8
  10.4 0.0 copy-done.1
  10.4 0.0 copy-done
  10.4 0.3 multiply_reduce_fusion
  10.7 0.0 copy-done.2
  10.7 3.9 %convolution_convert_fusion.1 = bf16[640,4096]{1,0:T(8,128)(2,1)} fusion(pred[640,64]{0,1:T(8,128)(4,1)S(1)} %fusion.8, bf16[64,4096]{1,0:T(8,128)(2,1)S(1)} %copy-done, bf16[64,4096]{1,0:T(8,128)(2,1)S(1)} %copy-done.1, f32[4096]{0:T(1024)S(1)} %copy-done.2, f32[64]{0:T(128)S(1)} %add_rsqrt_fusion), kind=kOutput, calls=%fused_computation.4 | convolution fusion | flops 339738624 | bytes 6349056 | tf_op jit(solution)/shard_map/dot_general | solution.py:35
  14.6 7.1 %all-to-all-start = ((bf16[16,40,4096]{2,1,0:T(8,128)(2,1)}), bf16[16,40,4096]{2,1,0:T(8,128)(2,1)}, u32[]{:S(2)}, u32[]{:S(2)}) async-start(bf16[16,40,4096]{2,1,0:T(8,128)(2,1)} %bitcast.44), calls=%async_computation | async-start | bytes 10485760 | tf_op jit(solution)/shard_map/all_to_all | solution.py:44
  21.8 0.0 all-gather.8.cloned.1.call-start
  21.8 0.7 all-gather.8.cloned.1.call-update
  22.5 4.4 %all-gather.4.cloned.1.call-done = bf16[1,4096,768]{2,1,0:T(8,128)(2,1)} async-done(((bf16[1,4096,384]{2,1,0:T(8,128)(2,1)}), bf16[1,4096,768]{2,1,0:T(8,128)(2,1)}) %all-gather.4.cloned.1.call-update) | async-done | bytes 6291472 | tf_op jit(solution)/shard_map/all_gather | solution.py:38
  26.9 113.0 %all-to-all-done = bf16[16,40,4096]{2,1,0:T(8,128)(2,1)} async-done(((bf16[16,40,4096]{2,1,0:T(8,128)(2,1)}), bf16[16,40,4096]{2,1,0:T(8,128)(2,1)}, u32[]{:S(2)}, u32[]{:S(2)}) %all-to-all-start) | async-done | bytes 5242912 | tf_op jit(solution)/shard_map/all_to_all | solution.py:44
  139.9 9.9 %fusion.4 = f32[640,768]{1,0:T(8,128)} fusion(bf16[640,4096]{1,0:T(8,128)(2,1)} %bitcast.2, bf16[1,4096,768]{2,1,0:T(8,128)(2,1)} %all-gather.4.cloned.1.call-done), kind=kOutput, calls=%fused_computation.8 | convolution fusion | flops 4026531840 | bytes 13500416 | tf_op jit(solution)/shard_map/dot_general | solution.py:10
  149.8 0.0 all-gather.6.cloned.1.call-done
  149.8 9.2 %multiply_convert_fusion = bf16[640,768]{1,0:T(8,128)(2,1)S(1)} fusion(f32[640,768]{1,0:T(8,128)} %fusion.4, bf16[640,4096]{1,0:T(8,128)(2,1)} %bitcast.2, bf16[1,4096,768]{2,1,0:T(8,128)(2,1)} %all-gather.6.cloned.1.call-done), kind=kOutput, calls=%fused_computation.10 | convolution fusion | flops 4029480960 | bytes 14483456 | tf_op jit(solution)/shard_map/dot_general | solution.py:11
  159.0 0.0 all-gather.8.cloned.1.call-done
  159.0 8.8 %convolution_convert_fusion = bf16[16,40,4096]{2,1,0:T(8,128)(2,1)} fusion(bf16[16,40,768]{2,1,0:T(8,128)(2,1)S(1)} %bitcast.47, bf16[1,768,4096]{2,1,0:T(8,128)(2,1)} %all-gather.8.cloned.1.call-done), kind=kOutput, calls=%fused_computation.3 | convolution fusion | flops 4029153280 | bytes 12517376 | tf_op jit(solution)/shard_map/dot_general | solution.py:13
  167.8 0.0 copy-start.4
  167.8 5.6 %all-to-all-start.1 = ((bf16[16,40,4096]{2,1,0:T(8,128)(2,1)}), bf16[16,40,4096]{2,1,0:T(8,128)(2,1)}, u32[]{:S(2)}, u32[]{:S(2)}) async-start(bf16[16,40,4096]{2,1,0:T(8,128)(2,1)} %convolution_convert_fusion), calls=%async_computation.1 | async-start | bytes 10485760 | tf_op jit(solution)/shard_map/all_to_all | solution.py:42
  173.4 0.1 mul.67
  173.5 0.0 copy-done.4
  173.5 0.1 copy.20
  173.6 115.1 %all-to-all-done.1 = bf16[16,40,4096]{2,1,0:T(8,128)(2,1)} async-done(((bf16[16,40,4096]{2,1,0:T(8,128)(2,1)}), bf16[16,40,4096]{2,1,0:T(8,128)(2,1)}, u32[]{:S(2)}, u32[]{:S(2)}) %all-to-all-start.1) | async-done | bytes 5242912 | tf_op jit(solution)/shard_map/all_to_all | solution.py:42
  288.7 11.8 %gather_fusion = bf16[512,4096]{1,0:T(8,128)(2,1)} fusion(bf16[640,4096]{1,0:T(8,128)(2,1)} %bitcast.8, s32[1024]{0:T(1024)S(1)} %pad_clamp_fusion), kind=kCustom, calls=%fused_computation | custom fusion | bytes 8390656 | tf_op jit(solution)/shard_map/gather | solution.py:55
  300.5 5.7 %fusion = f32[64,4096]{1,0:T(8,128)S(1)} fusion(bf16[512,4096]{1,0:T(8,128)(2,1)} %gather_fusion, f32[64,8]{1,0:T(8,128)S(1)} %copy.20), kind=kLoop, calls=%fused_computation.2 | loop fusion | flops 6029312 | bytes 5244928 | tf_op jit(solution)/shard_map/reduce_sum | solution.py:56
  306.2 1.0 add_convert_fusion
  (7 shorter events, 0.1 us)
Async XLA Ops:
  6.5 1.5 copy-start.3
  6.5 3.9 %copy-start.1 = (bf16[64,4096]{1,0:T(8,128)(2,1)S(1)}, bf16[64,4096]{1,0:T(8,128)(2,1)}, u32[]{:S(2)}) copy-start(bf16[64,4096]{1,0:T(8,128)(2,1)} %param.8) | copy-start | bytes 1572868
  6.5 3.9 %copy-start = (bf16[64,4096]{1,0:T(8,128)(2,1)S(1)}, bf16[64,4096]{1,0:T(8,128)(2,1)}, u32[]{:S(2)}) copy-start(bf16[64,4096]{1,0:T(8,128)(2,1)} %param.9) | copy-start | bytes 1572868
  6.5 4.2 %copy-start.2 = (f32[4096]{0:T(1024)S(1)}, f32[4096]{0:T(1024)}, u32[]{:S(2)}) copy-start(f32[4096]{0:T(1024)} %param.10) | copy-start | bytes 49156
  6.5 20.3 %all-gather.4.cloned.1.call-start = ((), (), s32[]{:S(2)}) async-start(), calls=%async_computation.2 | async-start | bytes 9437184 | tf_op jit(solution)/shard_map/all_gather | solution.py:38
  7.3 142.5 %all-gather.6.cloned.1.call-start = ((), (), s32[]{:S(2)}) async-start(), calls=%async_computation.3 | async-start | bytes 9437184 | tf_op jit(solution)/shard_map/all_gather | solution.py:39
  14.6 125.2 %all-to-all-start = ((bf16[16,40,4096]{2,1,0:T(8,128)(2,1)}), bf16[16,40,4096]{2,1,0:T(8,128)(2,1)}, u32[]{:S(2)}, u32[]{:S(2)}) async-start(bf16[16,40,4096]{2,1,0:T(8,128)(2,1)} %bitcast.44), calls=%async_computation | async-start | bytes 10485760 | tf_op jit(solution)/shard_map/all_to_all | solution.py:44
  21.8 137.2 %all-gather.8.cloned.1.call-start = ((), (), s32[]{:S(2)}) async-start(), calls=%async_computation.4 | async-start | bytes 9437184 | tf_op jit(solution)/shard_map/all_gather | solution.py:41
  167.8 5.7 %copy-start.4 = (f32[64,8]{0,1:T(8,128)S(1)}, f32[64,8]{0,1:T(8,128)}, u32[]{:S(2)}) copy-start(f32[64,8]{0,1:T(8,128)} %param.12) | copy-start | bytes 6148
  167.8 120.9 %all-to-all-start.1 = ((bf16[16,40,4096]{2,1,0:T(8,128)(2,1)}), bf16[16,40,4096]{2,1,0:T(8,128)(2,1)}, u32[]{:S(2)}, u32[]{:S(2)}) async-start(bf16[16,40,4096]{2,1,0:T(8,128)(2,1)} %convolution_convert_fusion), calls=%async_computation.1 | async-start | bytes 10485760 | tf_op jit(solution)/shard_map/all_to_all | solution.py:42
Sparse Core Ops, SparseCore 0:
  8.9 17.9 all-gather.3
  28.4 17.7 all-gather.5
  47.7 17.9 all-gather.7
where the time goes:
time: 314 us
  waiting for transfers between devices  235 us (75%)
  matrix products  31.8 us (10%)
  between operations  13.2 us (4%)
  starting transfers between devices  12.9 us (4%)
  local copies, waits for them, and re-layouts  12.6 us (4%)
  other arithmetic  8.71 us (3%)
    all_to_all x1, waiting for transfers between devices, shards(): lax.all_to_all(run_expert(lax.all_to_all(packed, 'expert', split_axis=0,...  115 us
    all_to_all x1, waiting for transfers between devices, shards(): lax.all_to_all(packed, 'expert', split_axis=0, concat_axis=0, tiled=True)  113 us
    gather x1, local copies, waits for them, and re-layouts, shards(): taken = returned[slot_of].reshape(rows, top, width)  11.8 us
    dot_general x1, matrix products, run_expert(): gate = jnp.dot(flat_rows, gate_part, preferred_element_type=jnp.float32)  9.91 us
    dot_general x1, matrix products, run_expert(): up = jnp.dot(flat_rows, up_part, preferred_element_type=jnp.float32)  9.18 us
    dot_general x1, matrix products, run_expert(): result = jnp.dot(hidden, down_part, preferred_element_type=jnp.float32)  8.81 us
    all_to_all x1, starting transfers between devices, shards(): lax.all_to_all(packed, 'expert', split_axis=0, concat_axis=0, tiled=True)  7.14 us
  transfers between devices with their start and end apart: 5, of which 3 were waited for; matrix products, arithmetic and copies ran while one was open for 8% of the time, Pallas kernels for 0%

commit v1 on v0

--- a/solution.py
+++ b/solution.py
@@ -14,15 +14,20 @@
     return result.reshape(inputs.shape)
 
 
-def shards(residual, attn_out, norm_gain, routes, mixing, gate_w, up_w, down_w):
+def normalise(residual, attn_out, norm_gain):
+    stream = residual.astype(jnp.float32) + attn_out.astype(jnp.float32)
+    square = jnp.mean(stream * stream, axis=1, keepdims=True)
+    normed = (stream * lax.rsqrt(square + 1e-06) * norm_gain[None, :]).astype(jnp.bfloat16)
+    return stream, normed
+
+
+def sparse_shards(residual, attn_out, norm_gain, routes, mixing, gate_w, up_w, down_w):
     experts = lax.axis_size("expert")
     rows, top = routes.shape
     width = residual.shape[1]
     capacity = max(2, 5 * rows * top // (4 * experts))
     slots = experts * capacity
-    stream = residual.astype(jnp.float32) + attn_out.astype(jnp.float32)
-    square = jnp.mean(stream * stream, axis=1, keepdims=True)
-    normed = (stream * lax.rsqrt(square + 1e-06) * norm_gain[None, :]).astype(jnp.bfloat16)
+    stream, normed = normalise(residual, attn_out, norm_gain)
     flat_routes = routes.reshape(-1)
     onehot = (flat_routes[:, None] == jnp.arange(experts, dtype=jnp.int32)[None, :]).astype(
         jnp.int32
@@ -57,6 +62,36 @@
     return (stream + mixed).astype(jnp.bfloat16)
 
 
+def dense_shards(residual, attn_out, norm_gain, routes, mixing, gate_w, up_w, down_w):
+    experts = lax.axis_size("expert")
+    me = lax.axis_index("expert")
+    stream, normed = normalise(residual, attn_out, norm_gain)
+    hit = routes[:, :, None] == jnp.arange(experts, dtype=jnp.int32)[None, None, :]
+    share = jnp.sum(jnp.where(hit, mixing[:, :, None], 0.0), axis=1)
+    shares = lax.all_gather(share, "expert", axis=0, tiled=True)
+    tokens = lax.all_gather(normed, "expert", axis=0, tiled=True)
+    gate_full = lax.all_gather(gate_w, "dp", axis=2, tiled=True)[0]
+    up_full = lax.all_gather(up_w, "dp", axis=2, tiled=True)[0]
+    down_full = lax.all_gather(down_w, "dp", axis=1, tiled=True)[0]
+    own = jnp.sum(
+        jnp.where(jnp.arange(experts)[None, :] == me, shares, 0.0), axis=1, keepdims=True
+    )
+    gate = jnp.dot(tokens, gate_full, preferred_element_type=jnp.float32)
+    up = jnp.dot(tokens, up_full, preferred_element_type=jnp.float32)
+    hidden = (jax.nn.silu(gate) * up * own).astype(jnp.bfloat16)
+    result = jnp.dot(hidden, down_full, preferred_element_type=jnp.float32)
+    mixed = lax.psum_scatter(
+        result.astype(jnp.bfloat16), "expert", scatter_dimension=0, tiled=True
+    )
+    return (stream + mixed.astype(jnp.float32)).astype(jnp.bfloat16)
+
+
+def shards(residual, attn_out, norm_gain, routes, *rest):
+    experts = lax.axis_size("expert")
+    plan = dense_shards if 2 * routes.shape[1] >= experts else sparse_shards
+    return plan(residual, attn_out, norm_gain, routes, *rest)
+
+
 def solution(mesh):
     return jax.shard_map(
         shards,

time: 314 us -> 381 us (1.21)
  the two profiles are of different devices: /device:TPU:14 before, /device:TPU:0 now
where the time goes in v1:
time: 381 us; the launch traced here: 379 us
  waiting for transfers between devices  282 us (74%)
  blocking collectives  43.6 us (11%)
  matrix products  34.2 us (9%)
  between operations  13.2 us (3%)
  other arithmetic  5.82 us (2%)
    reduce_scatter x1, waiting for transfers between devices, dense_shards(): lax.psum_scatter(result.astype(jnp.bfloat16), 'expert', scatter_dimension...  179 us
    all_gather x1, waiting for transfers between devices, dense_shards(): tokens = lax.all_gather(normed, 'expert', axis=0, tiled=True)  88.3 us
    all_gather x1, blocking collectives, dense_shards(): shares = lax.all_gather(share, 'expert', axis=0, tiled=True)  43.6 us
    dot_general x1, matrix products, dense_shards(): gate = jnp.dot(tokens, gate_full, preferred_element_type=jnp.float32)  12.1 us
    dot_general x1, matrix products, dense_shards(): result = jnp.dot(hidden, down_full, preferred_element_type=jnp.float32)  11.2 us
    dot_general x1, matrix products, dense_shards(): up = jnp.dot(tokens, up_full, preferred_element_type=jnp.float32)  10.9 us
  transfers between devices with their start and end apart: 5, of which 4 were waited for; matrix products, arithmetic and copies ran while one was open for 7% of the time, Pallas kernels for 0%

profile of v1, /device:TPU:0, one launch (start us, length us, event | category | flops | bytes accessed | tf_op | source)
XLA Modules:
  0.0 379.3 jit_solution(10033263787395311019)
XLA Ops:
  6.5 0.0 copy-start.3
  6.5 0.0 copy-start.2
  6.5 0.0 all-gather.10.cloned.1.call-start
  6.5 0.7 all-gather.10.cloned.1.call-update
  7.3 0.0 all-gather.6.cloned.1.call-start
  7.3 1.5 multiply_reduce_fusion
  8.8 2.2 multiply_convert_fusion.1
  11.0 0.0 all-gather.6.cloned.1.call-update
  11.0 0.0 all-gather.8.cloned.1.call-start
  11.1 0.7 all-gather.8.cloned.1.call-update
  11.8 0.0 all-gather.12.cloned.1.call-start
  11.8 0.5 all-gather.12.cloned.1.call-update
  12.3 0.0 reduce-scatter.2.cloned.1.call-start
  12.4 0.0 copy-done.3
  12.4 0.0 copy-done.2
  12.4 43.6 %all-gather = f32[16,64,16]{1,2,0:T(8,128)S(1)} all-gather(f32[1,64,16]{1,2,0:T(8,128)S(1)} %bitcast.17), channel_id=1, replica_groups=mesh['dp'=2,'expert'=16] {'expert'}, dimensions={0}, use_global_device_ids=true | all-gather | bytes 69632 | tf_op jit(solution)/shard_map/all_gather | solution.py:71
  56.1 0.1 reshape.18
  56.2 0.1 select_reduce_fusion
  56.3 0.0 all-gather.10.cloned.1.call-done
  56.3 88.3 %all-gather.6.cloned.1.call-done = bf16[1024,4096]{1,0:T(8,128)(2,1)} async-done(((bf16[64,4096]{1,0:T(8,128)(2,1)}), bf16[1024,4096]{1,0:T(8,128)(2,1)}) %all-gather.6.cloned.1.call-update) | async-done | bytes 8388624 | tf_op jit(solution)/shard_map/all_gather | solution.py:72
  144.7 10.9 %fusion.1 = f32[1024,768]{1,0:T(8,128)S(1)} fusion(bf16[1024,4096]{1,0:T(8,128)(2,1)} %all-gather.6.cloned.1.call-done, bf16[1,4096,768]{2,1,0:T(8,128)(2,1)} %all-gather.10.cloned.1.call-done), kind=kOutput, calls=%fused_computation.2 | convolution fusion | flops 6442450944 | bytes 17825792 | tf_op jit(solution)/shard_map/dot_general | solution.py:80
  155.6 5.4 %all-gather.8.cloned.1.call-done = bf16[1,4096,768]{2,1,0:T(8,128)(2,1)} async-done(((bf16[1,4096,384]{2,1,0:T(8,128)(2,1)}), bf16[1,4096,768]{2,1,0:T(8,128)(2,1)}) %all-gather.8.cloned.1.call-update) | async-done | bytes 6291472 | tf_op jit(solution)/shard_map/all_gather | solution.py:73
  161.0 12.1 %multiply_convert_fusion = bf16[1024,768]{1,0:T(8,128)(2,1)} fusion(f32[1024,768]{1,0:T(8,128)S(1)} %fusion.1, bf16[1024,4096]{1,0:T(8,128)(2,1)} %all-gather.6.cloned.1.call-done, bf16[1,4096,768]{2,1,0:T(8,128)(2,1)} %all-gather.8.cloned.1.call-done, f32[1024]{0:T(1024)S(1)} %select_reduce_fusion), kind=kOutput, calls=%fused_computation.6 | convolution fusion | flops 6447955968 | bytes 19402752 | tf_op jit(solution)/shard_map/dot_general | solution.py:79
  173.1 7.2 %all-gather.12.cloned.1.call-done = bf16[1,768,4096]{2,1,0:T(8,128)(2,1)} async-done(((bf16[1,384,4096]{2,1,0:T(8,128)(2,1)}), bf16[1,768,4096]{2,1,0:T(8,128)(2,1)}) %all-gather.12.cloned.1.call-update) | async-done | bytes 6291472 | tf_op jit(solution)/shard_map/all_gather | solution.py:75
  180.3 11.2 %convolution_convert_fusion = bf16[1024,4096]{1,0:T(8,128)(2,1)} fusion(bf16[1024,768]{1,0:T(8,128)(2,1)} %multiply_convert_fusion, bf16[1,768,4096]{2,1,0:T(8,128)(2,1)} %all-gather.12.cloned.1.call-done), kind=kOutput, calls=%fused_computation | convolution fusion | flops 6446645248 | bytes 16252928 | tf_op jit(solution)/shard_map/dot_general | solution.py:82
  191.5 0.0 copy-start
  191.5 0.0 copy-start.1
  191.5 0.0 reduce-scatter.2.cloned.1.call-update
  191.6 179.2 %reduce-scatter.2.cloned.1.call-done = bf16[64,4096]{1,0:T(8,128)(2,1)} async-done(((bf16[1024,4096]{1,0:T(8,128)(2,1)}), bf16[64,4096]{1,0:T(8,128)(2,1)}) %reduce-scatter.2.cloned.1.call-update) | async-done | bytes 524304 | tf_op jit(solution)/shard_map/reduce_scatter | solution.py:83
  370.7 0.0 copy-done
  370.7 0.0 copy-done.1
  370.7 2.0 add_convert_fusion
  (4 shorter events, 0.1 us)
Async XLA Ops:
  6.5 5.9 %copy-start.3 = (s32[64,8]{0,1:T(8,128)S(1)}, s32[64,8]{0,1:T(8,128)}, u32[]{:S(2)}) copy-start(s32[64,8]{0,1:T(8,128)} %param.11) | copy-start | bytes 6148
  6.5 5.9 %copy-start.2 = (f32[64,8]{0,1:T(8,128)S(1)}, f32[64,8]{0,1:T(8,128)}, u32[]{:S(2)}) copy-start(f32[64,8]{0,1:T(8,128)} %param.12) | copy-start | bytes 6148
  6.5 49.8 %all-gather.10.cloned.1.call-start = ((), (), s32[]{:S(2)}) async-start(), calls=%async_computation.3 | async-start | bytes 9437184 | tf_op jit(solution)/shard_map/all_gather | solution.py:74
  7.3 137.4 %all-gather.6.cloned.1.call-start = ((), (), s32[]{:S(2)}) async-start(), calls=%async_computation.1 | async-start | bytes 8912896 | tf_op jit(solution)/shard_map/all_gather | solution.py:72
  11.0 150.0 %all-gather.8.cloned.1.call-start = ((), (), s32[]{:S(2)}) async-start(), calls=%async_computation.2 | async-start | bytes 9437184 | tf_op jit(solution)/shard_map/all_gather | solution.py:73
  11.8 168.6 %all-gather.12.cloned.1.call-start = ((), (), s32[]{:S(2)}) async-start(), calls=%async_computation.4 | async-start | bytes 9437184 | tf_op jit(solution)/shard_map/all_gather | solution.py:75
  12.3 358.4 %reduce-scatter.2.cloned.1.call-start = ((), (), s32[]{:S(2)}) async-start(), calls=%async_computation.5 | async-start | bytes 8912896 | tf_op jit(solution)/shard_map/reduce_scatter | solution.py:83
  191.5 179.2 %copy-start = (bf16[64,4096]{1,0:T(8,128)(2,1)S(1)}, bf16[64,4096]{1,0:T(8,128)(2,1)}, u32[]{:S(2)}) copy-start(bf16[64,4096]{1,0:T(8,128)(2,1)} %param.9) | copy-start | bytes 1572868
  191.5 179.2 %copy-start.1 = (bf16[64,4096]{1,0:T(8,128)(2,1)S(1)}, bf16[64,4096]{1,0:T(8,128)(2,1)}, u32[]{:S(2)}) copy-start(bf16[64,4096]{1,0:T(8,128)(2,1)} %param.8) | copy-start | bytes 1572868
Sparse Core Ops, SparseCore 0:
  8.9 19.2 all-gather.9
  31.0 113.6 all-gather.5
  146.2 14.7 all-gather.7
  162.4 17.9 all-gather.11
  191.7 179.0 reduce-scatter.1

commit v2 on v0

--- a/solution.py
+++ b/solution.py
@@ -1,6 +1,10 @@
+import functools
+
 import jax
 import jax.numpy as jnp
 from jax import lax
+from jax.experimental import pallas as pl
+from jax.experimental.pallas import tpu as pltpu
 from jax.sharding import PartitionSpec as P
 
 
@@ -14,15 +18,20 @@
     return result.reshape(inputs.shape)
 
 
-def shards(residual, attn_out, norm_gain, routes, mixing, gate_w, up_w, down_w):
+def normalise(residual, attn_out, norm_gain):
+    stream = residual.astype(jnp.float32) + attn_out.astype(jnp.float32)
+    square = jnp.mean(stream * stream, axis=1, keepdims=True)
+    normed = (stream * lax.rsqrt(square + 1e-06) * norm_gain[None, :]).astype(jnp.bfloat16)
+    return stream, normed
+
+
+def sparse_shards(residual, attn_out, norm_gain, routes, mixing, gate_w, up_w, down_w):
     experts = lax.axis_size("expert")
     rows, top = routes.shape
     width = residual.shape[1]
     capacity = max(2, 5 * rows * top // (4 * experts))
     slots = experts * capacity
-    stream = residual.astype(jnp.float32) + attn_out.astype(jnp.float32)
-    square = jnp.mean(stream * stream, axis=1, keepdims=True)
-    normed = (stream * lax.rsqrt(square + 1e-06) * norm_gain[None, :]).astype(jnp.bfloat16)
+    stream, normed = normalise(residual, attn_out, norm_gain)
     flat_routes = routes.reshape(-1)
     onehot = (flat_routes[:, None] == jnp.arange(experts, dtype=jnp.int32)[None, :]).astype(
         jnp.int32
@@ -57,6 +66,360 @@
     return (stream + mixed).astype(jnp.bfloat16)
 
 
+CHUNKS = 2
+MESH = pl.DeviceIdType.MESH
+
+
+def fused_kernel(
+    experts, x_ref, res_ref, att_ref, gate_ref, up_ref, down_ref, o_ref,
+    tok, part, wg, wu, wd, hid, rb, ra, rz, fin, wsem, gsend, grecv, ssend, srecv,
+):
+    rows, width = o_ref.shape
+    full = x_ref.shape[1]
+    take = rows // CHUNKS
+    chain = experts // 4
+    half = width // 2
+    mine = gate_ref.shape[1]
+    hidden = wg.shape[1]
+    htile = 256 if hidden % 256 == 0 else 128
+    wtile = 512 if half % 512 == 0 else 128
+    dp, me = lax.axis_index("dp"), lax.axis_index("expert")
+    z, y, x = me // 4, (me // 2) % 2, me % 2
+    more, less = z + 1 < chain, z > 0
+    coords = ((y, x, 2, 1), (x, y, 1, 2))
+
+    def slot(p, zz, aa, bb):
+        return zz * 4 + aa * coords[p][2] + bb * coords[p][3]
+
+    def span(j):
+        return pl.ds(pl.multiple_of(j * take, take), take)
+
+    gcols = (pl.ds(0, half), pl.ds(half, full - half))
+    scols = (pl.ds(0, half), pl.ds(half, half))
+
+    barrier = pltpu.get_barrier_semaphore()
+    pl.semaphore_signal(barrier, inc=1, device_id={"dp": 1 - dp}, device_id_type=MESH)
+    for p in range(2):
+        a, b = coords[p][0], coords[p][1]
+        pl.semaphore_signal(
+            barrier, inc=1, device_id={"expert": slot(p, z, a, 1 - b)}, device_id_type=MESH
+        )
+
+    @pl.when(more)
+    def _():
+        pl.semaphore_signal(barrier, inc=1, device_id={"expert": me + 4}, device_id_type=MESH)
+
+    @pl.when(less)
+    def _():
+        pl.semaphore_signal(barrier, inc=1, device_id={"expert": me - 4}, device_id_type=MESH)
+
+    pl.semaphore_wait(barrier, 3 + jnp.where(more, 1, 0) + jnp.where(less, 1, 0))
+
+    pending = []
+    used = {"g": 0, "s": 0}
+
+    def send(kind, src, dst, recv, target, cond=None):
+        sems = gsend if kind == "g" else ssend
+        n = used[kind]
+        used[kind] = n + 1
+
+        def copy():
+            return pltpu.make_async_remote_copy(
+                src_ref=src, dst_ref=dst, send_sem=sems.at[n], recv_sem=recv,
+                device_id=target, device_id_type=MESH,
+            )
+
+        def go():
+            copy().start()
+
+        def end():
+            copy().wait_send()
+
+        if cond is None:
+            go()
+        else:
+            pl.when(cond)(go)
+        pending.append((cond, end))
+
+    def arrived(dst, recv):
+        pltpu.make_async_remote_copy(
+            src_ref=dst, dst_ref=dst, send_sem=wsem.at[0], recv_sem=recv,
+            device_id={"dp": 1 - dp}, device_id_type=MESH,
+        ).wait_recv()
+
+    columns = pl.ds(pl.multiple_of(dp * mine, 128), mine)
+    lines = pl.ds(pl.multiple_of(dp * mine, 128), mine)
+    others = pl.ds(pl.multiple_of((1 - dp) * mine, 128), mine)
+    pairs = (
+        (gate_ref, wg.at[:, columns], wg.at[:, others]),
+        (up_ref, wu.at[:, columns], wu.at[:, others]),
+        (down_ref, wd.at[lines, :], wd.at[others, :]),
+    )
+
+    def local(i):
+        return pltpu.make_async_copy(pairs[i][0], pairs[i][1], wsem.at[1 + i])
+
+    def remote(i):
+        return pltpu.make_async_remote_copy(
+            src_ref=pairs[i][0], dst_ref=pairs[i][1], send_sem=wsem.at[4 + i],
+            recv_sem=wsem.at[7 + i], device_id={"dp": 1 - dp}, device_id_type=MESH,
+        )
+
+    def start_weights():
+        for i in range(3):
+            remote(i).start()
+            local(i).start()
+
+    def wait_weights(i):
+        local(i).wait()
+        arrived(pairs[i][2], wsem.at[7 + i])
+        remote(i).wait_send()
+
+    def gather_send(c, p, src, j, target, cond=None):
+        send("g", src, tok.at[c, span(j), gcols[p]], grecv.at[c, p, j], {"expert": target}, cond)
+
+    def gather_start(c, p):
+        a, b = coords[p][0], coords[p][1]
+        src = x_ref.at[pl.ds(c * take, take), gcols[p]]
+        gather_send(c, p, src, me, slot(p, z, 1 - a, b))
+        gather_send(c, p, src, me, me + 4, more)
+        gather_send(c, p, src, me, me - 4, less)
+        gather_send(c, p, src, me, slot(p, z, a, 1 - b))
+
+    def gather_wait(c, p, j):
+        arrived(tok.at[c, span(j), gcols[p]], grecv.at[c, p, j])
+
+    def gather_side(c, p, zz, onward, target, cond):
+        a, b = coords[p][0], coords[p][1]
+        j = slot(p, zz, a, b)
+        pl.when(cond)(lambda: gather_wait(c, p, j))
+        src = tok.at[c, span(j), gcols[p]]
+        gather_send(c, p, src, j, slot(p, z, 1 - a, b), cond)
+        gather_send(c, p, src, j, target, jnp.logical_and(cond, onward))
+        gather_send(c, p, src, j, slot(p, z, a, 1 - b), cond)
+
+    def gather_chain(c, p, s):
+        gather_side(c, p, z - s, more, me + 4, z - s >= 0)
+        gather_side(c, p, z + s, less, me - 4, z + s < chain)
+
+    def gather_second(c, p, s):
+        a, b = coords[p][0], coords[p][1]
+        sides = ((z, None),) if s == 0 else ((z - s, z - s >= 0), (z + s, z + s < chain))
+        for zz, cond in sides:
+            j = slot(p, zz, 1 - a, b)
+            if cond is None:
+                gather_wait(c, p, j)
+            else:
+                pl.when(cond)(functools.partial(gather_wait, c, p, j))
+            src = tok.at[c, span(j), gcols[p]]
+            gather_send(c, p, src, j, slot(p, z, a, 1 - b), cond)
+
+    def gather_last(c, p):
+        a, b = coords[p][0], coords[p][1]
+        for zz in range(chain):
+            for aa in range(2):
+                gather_wait(c, p, slot(p, zz, aa, 1 - b))
+
+    def gather_events(c):
+        def both(f, *rest):
+            return lambda: [f(c, p, *rest) for p in range(2)]
+
+        def own():
+            tok[c, span(me), :] = x_ref[pl.ds(c * take, take), :]
+
+        events = [lambda: (both(gather_start)(), own())]
+        for s in range(chain):
+            if s > 0:
+                events.append(both(gather_chain, s))
+            events.append(both(gather_second, s))
+        events.append(both(gather_last))
+        return events
+
+    def shares(c):
+        extra = tok[c, :, pl.ds(width, full - width)].astype(jnp.float32)
+        lane = lax.broadcasted_iota(jnp.int32, extra.shape, 1)
+        keep = jnp.logical_or(lane == me, lane == experts + me)
+        return jnp.sum(jnp.where(keep, extra, 0.0), axis=1, keepdims=True)
+
+    def expert_in(c, n):
+        cut = pl.ds(n * htile, htile)
+        values = tok[c, :, pl.ds(0, width)]
+        gate = jnp.dot(values, wg[:, cut], preferred_element_type=jnp.float32)
+        up = jnp.dot(values, wu[:, cut], preferred_element_type=jnp.float32)
+        act = gate / (1.0 + jnp.exp(-gate)) * up * shares(c)
+        hid[:, cut] = act.astype(hid.dtype)
+
+    def expert_out(c, p):
+        @pl.loop(0, half // wtile)
+        def _(n):
+            cut = pl.ds(pl.multiple_of(p * half + n * wtile, wtile), wtile)
+            done = jnp.dot(hid[...], wd[:, cut], preferred_element_type=jnp.float32)
+            part[c, :, cut] = done.astype(part.dtype)
+
+    def expert_events(c):
+        events = []
+        for n in range(hidden // htile):
+            events.append(functools.partial(expert_in, c, n))
+        for p in range(2):
+            events.append(lambda p=p: (expert_out(c, p), scatter_first(c, p)))
+        return events
+
+    def scatter_first(c, p):
+        a, b = coords[p][0], coords[p][1]
+        for aa in (1 - a, a):
+            for zz in range(chain):
+                src = part.at[c, span(slot(p, zz, aa, 1 - b)), scols[p]]
+                k = zz * 2 + aa
+                send("s", src, rb.at[c, p, k], srecv.at[c, p, k],
+                     {"expert": slot(p, z, a, 1 - b)})
+
+    def scatter_second(c, p, zz):
+        a, b = coords[p][0], coords[p][1]
+        k = zz * 2 + 1 - a
+        arrived(rb.at[c, p, k], srecv.at[c, p, k])
+        here = (c, span(slot(p, zz, 1 - a, b)), scols[p])
+        both = part[here].astype(jnp.float32) + rb[c, p, k].astype(jnp.float32)
+        part[here] = both.astype(part.dtype)
+        send("s", part.at[here], ra.at[c, p, zz], srecv.at[c, p, 2 * chain + zz],
+             {"expert": slot(p, z, 1 - a, b)})
+
+    def summed(c, p, zz):
+        a, b = coords[p][0], coords[p][1]
+        k = zz * 2 + a
+        arrived(rb.at[c, p, k], srecv.at[c, p, k])
+        arrived(ra.at[c, p, zz], srecv.at[c, p, 2 * chain + zz])
+        own = part[c, span(slot(p, zz, a, b)), scols[p]].astype(jnp.float32)
+        return own + rb[c, p, k].astype(jnp.float32) + ra[c, p, zz].astype(jnp.float32)
+
+    def passing(c, p, way, zz):
+        k = (3 + way) * chain + zz
+        arrived(rz.at[c, p, way, zz], srecv.at[c, p, k])
+        return rz[c, p, way, zz].astype(jnp.float32)
+
+    def scatter_side(c, p, way, zz, cond, behind, target):
+        a, b = coords[p][0], coords[p][1]
+        here = (c, span(slot(p, zz, a, b)), scols[p])
+
+        @pl.when(cond)
+        def _():
+            part[here] = summed(c, p, zz).astype(part.dtype)
+
+        @pl.when(jnp.logical_and(cond, behind))
+        def _():
+            more_of = part[here].astype(jnp.float32) + passing(c, p, way, zz)
+            part[here] = more_of.astype(part.dtype)
+
+        send("s", part.at[here], rz.at[c, p, way, zz],
+             srecv.at[c, p, (3 + way) * chain + zz], {"expert": target}, cond)
+
+    def scatter_chain(c, p, s):
+        scatter_side(c, p, 0, z + s, z + s < chain, less, me + 4)
+        scatter_side(c, p, 1, z - s, z - s >= 0, more, me - 4)
+
+    def scatter_last(c, p):
+        lines = pl.ds(c * take, take)
+        total = summed(c, p, z)
+        stream = res_ref[lines, scols[p]].astype(jnp.float32) + att_ref[
+            lines, scols[p]
+        ].astype(jnp.float32)
+        fin[:, :] = total
+
+        @pl.when(less)
+        def _():
+            fin[:, :] += passing(c, p, 0, z)
+
+        @pl.when(more)
+        def _():
+            fin[:, :] += passing(c, p, 1, z)
+
+        o_ref[lines, scols[p]] = (stream + fin[:, :]).astype(o_ref.dtype)
+
+    def scatter_events(c):
+        def both(f, *rest):
+            return lambda: [f(c, p, *rest) for p in range(2)]
+
+        events = [both(scatter_second, zz) for zz in range(chain)]
+        events += [both(scatter_chain, s) for s in range(chain - 1, 0, -1)]
+        events.append(both(scatter_last))
+        return events
+
+    def merged(first, second):
+        out = []
+        for i in range(max(len(first), len(second))):
+            out += first[i : i + 1] + second[i : i + 1]
+        return out
+
+    fetch = [gather_events(c) for c in range(CHUNKS)]
+    work = [expert_events(c) for c in range(CHUNKS)]
+    back = [scatter_events(c) for c in range(CHUNKS)]
+    order = fetch[0][:1] + [start_weights] + fetch[0][1:3] + fetch[1][:1] + fetch[0][3:]
+    order += [lambda: [wait_weights(i) for i in range(3)]]
+    order += merged(fetch[1][1:], work[0])
+    order += merged(work[1], back[0]) + back[1]
+    for event in order:
+        event()
+    for cond, end in pending:
+        if cond is None:
+            end()
+        else:
+            pl.when(cond)(end)
+
+
+def multicast_shards(residual, attn_out, norm_gain, routes, mixing, gate_w, up_w, down_w):
+    experts = lax.axis_size("expert")
+    rows, width = residual.shape
+    mine = gate_w.shape[2]
+    hidden = mine * lax.axis_size("dp")
+    lanes = -(-2 * experts // 128) * 128
+    full = width + lanes
+    take, chain = rows // CHUNKS, experts // 4
+    _, normed = normalise(residual, attn_out, norm_gain)
+    hit = routes[:, :, None] == jnp.arange(experts, dtype=jnp.int32)[None, None, :]
+    share = jnp.sum(jnp.where(hit, mixing[:, :, None], 0.0), axis=1)
+    high = lax.reduce_precision(share, 8, 7)
+    extra = jnp.concatenate([high, share - high], axis=1).astype(jnp.bfloat16)
+    extra = jnp.pad(extra, ((0, 0), (0, lanes - 2 * experts)))
+    packed = jnp.concatenate([normed, extra], axis=1)
+    bf16 = jnp.bfloat16
+    copies = 2 * CHUNKS * (4 + 6 * (chain - 1) + 1 + 2 * (chain - 1))
+    sums = 2 * CHUNKS * (3 * chain + 2 * (chain - 1))
+    vmem, anywhere = pl.BlockSpec(memory_space=pltpu.VMEM), pl.BlockSpec(memory_space=pl.ANY)
+    return pl.pallas_call(
+        functools.partial(fused_kernel, experts),
+        out_shape=jax.ShapeDtypeStruct((rows, width), bf16),
+        in_specs=[vmem] * 3 + [anywhere] * 3,
+        out_specs=vmem,
+        scratch_shapes=[
+            pltpu.VMEM((CHUNKS, experts * take, full), bf16),
+            pltpu.VMEM((CHUNKS, experts * take, width), bf16),
+            pltpu.VMEM((width, hidden), bf16),
+            pltpu.VMEM((width, hidden), bf16),
+            pltpu.VMEM((hidden, width), bf16),
+            pltpu.VMEM((experts * take, hidden), bf16),
+            pltpu.VMEM((CHUNKS, 2, 2 * chain, take, width // 2), bf16),
+            pltpu.VMEM((CHUNKS, 2, chain, take, width // 2), bf16),
+            pltpu.VMEM((CHUNKS, 2, 2, chain, take, width // 2), bf16),
+            pltpu.VMEM((take, width // 2), jnp.float32),
+            pltpu.SemaphoreType.DMA((10,)),
+            pltpu.SemaphoreType.DMA((copies,)),
+            pltpu.SemaphoreType.DMA((CHUNKS, 2, experts)),
+            pltpu.SemaphoreType.DMA((sums,)),
+            pltpu.SemaphoreType.DMA((CHUNKS, 2, 5 * chain)),
+        ],
+        compiler_params=pltpu.CompilerParams(
+            collective_id=0, has_side_effects=True, vmem_limit_bytes=66 * 1000 * 1000
+        ),
+    )(packed, residual, attn_out, gate_w[0], up_w[0], down_w[0])
+
+
+def shards(residual, attn_out, norm_gain, routes, *rest):
+    experts = lax.axis_size("expert")
+    paired = lax.axis_size("dp") == 2 and experts % 4 == 0 and residual.shape[0] % 32 == 0
+    wide = 2 * routes.shape[1] >= experts
+    plan = multicast_shards if paired and wide else sparse_shards
+    return plan(residual, attn_out, norm_gain, routes, *rest)
+
+
 def solution(mesh):
     return jax.shard_map(
         shards,

time: 314 us -> 187 us (0.60)
  the two profiles are of different devices: /device:TPU:14 before, /device:TPU:0 now
where the time goes in v2:
time: 187 us
  Pallas kernels  180 us (96%)
  other arithmetic  4.54 us (2%)
  local copies, waits for them, and re-layouts  2.03 us (1%)
    pallas_call x1, Pallas kernels, multicast_shards(): pl.pallas_call(functools.partial(fused_kernel, experts), out_shape=jax.Sh...  180 us

profile of v2, /device:TPU:0, one launch (start us, length us, event | category | flops | bytes accessed | tf_op | source)
XLA Modules:
  0.0 186.5 jit_solution(6978568420083913186)
XLA Ops:
  0.0 1.5 multiply_reduce_fusion
  1.5 0.7 select_reduce_fusion
  2.2 0.1 copy.14
  2.3 0.1 copy.13
  2.4 0.1 fusion.2
  2.5 1.4 multiply_convert_fusion
  3.9 0.8 pad_maximum_fusion.x_ref
  4.7 179.9 %shard_map.82 = bf16[64,4096]{1,0:T(8,128)(2,1)} custom-call(bf16[64,4224]{1,0:T(8,128)(2,1)} %pad_maximum_fusion.x_ref, bf16[64,4096]{1,0:T(8,128)(2,1)} %res_ref.1, bf16[64,4096]{1,0:T(8,128)(2,1)} %att_ref.1, bf16[4096,384]{1,0:T(8,128)(2,1)} %bitcast.3, bf16[4096,384]{1,0:T(8,128)(2,1)} %bitcast.4, bf16[384,4096]{1,0:T(8,128)(2,1)} %bitcast.5), custom_call_target="tpu_custom_call" | custom-call | tf_op jit(solution)/shard_map/pallas_call | solution.py:387
  184.7 1.9 %copy.17 = bf16[64,4096]{1,0:T(8,128)(2,1)} copy(bf16[64,4096]{1,0:T(8,128)(2,1)} %shard_map.82) | data formatting | bytes 1048576
  (3 shorter events, 0.0 us)

commit v3 on v2

--- a/solution.py
+++ b/solution.py
@@ -67,6 +67,7 @@
 
 
 CHUNKS = 2
+PARTS = 4
 MESH = pl.DeviceIdType.MESH
 
 
@@ -78,15 +79,17 @@
     full = x_ref.shape[1]
     take = rows // CHUNKS
     chain = experts // 4
-    half = width // 2
+    piece = width // PARTS
     mine = gate_ref.shape[1]
     hidden = wg.shape[1]
     htile = 256 if hidden % 256 == 0 else 128
-    wtile = 512 if half % 512 == 0 else 128
+    wtile = 512 if piece % 512 == 0 else 128
     dp, me = lax.axis_index("dp"), lax.axis_index("expert")
     z, y, x = me // 4, (me // 2) % 2, me % 2
     more, less = z + 1 < chain, z > 0
-    coords = ((y, x, 2, 1), (x, y, 1, 2))
+    coords = ((x, y, 1, 2), (y, x, 2, 1), (y, x, 2, 1), (x, y, 1, 2))
+    early, late = (0, 1), (2, 3)
+    every = early + late
 
     def slot(p, zz, aa, bb):
         return zz * 4 + aa * coords[p][2] + bb * coords[p][3]
@@ -94,12 +97,12 @@
     def span(j):
         return pl.ds(pl.multiple_of(j * take, take), take)
 
-    gcols = (pl.ds(0, half), pl.ds(half, full - half))
-    scols = (pl.ds(0, half), pl.ds(half, half))
+    scols = [pl.ds(p * piece, piece) for p in every]
+    gcols = scols[:-1] + [pl.ds(width - piece, full - width + piece)]
 
     barrier = pltpu.get_barrier_semaphore()
     pl.semaphore_signal(barrier, inc=1, device_id={"dp": 1 - dp}, device_id_type=MESH)
-    for p in range(2):
+    for p in late:
         a, b = coords[p][0], coords[p][1]
         pl.semaphore_signal(
             barrier, inc=1, device_id={"expert": slot(p, z, a, 1 - b)}, device_id_type=MESH
@@ -189,18 +192,30 @@
     def gather_wait(c, p, j):
         arrived(tok.at[c, span(j), gcols[p]], grecv.at[c, p, j])
 
-    def gather_side(c, p, zz, onward, target, cond):
-        a, b = coords[p][0], coords[p][1]
-        j = slot(p, zz, a, b)
+    def gather_turn(c, p):
+        a, b = coords[p][0], coords[p][1]
+        j = slot(p, z, 1 - a, b)
+        gather_wait(c, p, j)
+        src = tok.at[c, span(j), gcols[p]]
+        gather_send(c, p, src, j, me + 4, more)
+        gather_send(c, p, src, j, me - 4, less)
+        gather_send(c, p, src, j, slot(p, z, a, 1 - b))
+
+    def gather_side(c, p, zz, aa, onward, target, cond):
+        a, b = coords[p][0], coords[p][1]
+        j = slot(p, zz, aa, b)
         pl.when(cond)(lambda: gather_wait(c, p, j))
         src = tok.at[c, span(j), gcols[p]]
-        gather_send(c, p, src, j, slot(p, z, 1 - a, b), cond)
+        if p in late:
+            gather_send(c, p, src, j, slot(p, z, 1 - a, b), cond)
         gather_send(c, p, src, j, target, jnp.logical_and(cond, onward))
         gather_send(c, p, src, j, slot(p, z, a, 1 - b), cond)
 
     def gather_chain(c, p, s):
-        gather_side(c, p, z - s, more, me + 4, z - s >= 0)
-        gather_side(c, p, z + s, less, me - 4, z + s < chain)
+        a = coords[p][0]
+        for aa in (a, 1 - a) if p in early else (a,):
+            gather_side(c, p, z - s, aa, more, me + 4, z - s >= 0)
+            gather_side(c, p, z + s, aa, less, me - 4, z + s < chain)
 
     def gather_second(c, p, s):
         a, b = coords[p][0], coords[p][1]
@@ -220,19 +235,21 @@
             for aa in range(2):
                 gather_wait(c, p, slot(p, zz, aa, 1 - b))
 
+    def over(parts, f, *rest):
+        return lambda: [f(rest[0], p, *rest[1:]) for p in parts]
+
     def gather_events(c):
-        def both(f, *rest):
-            return lambda: [f(c, p, *rest) for p in range(2)]
-
         def own():
             tok[c, span(me), :] = x_ref[pl.ds(c * take, take), :]
 
-        events = [lambda: (both(gather_start)(), own())]
-        for s in range(chain):
-            if s > 0:
-                events.append(both(gather_chain, s))
-            events.append(both(gather_second, s))
-        events.append(both(gather_last))
+        events = [lambda: (over(every, gather_start, c)(), own())]
+        events.append(over(early, gather_turn, c))
+        for s in range(1, chain):
+            events.append(over(late, gather_chain, c, s))
+            events.append(over(late, gather_second, c, s - 1))
+            events.append(over(early, gather_chain, c, s))
+        events.append(over(late, gather_second, c, chain - 1))
+        events.append(over(every, gather_last, c))
         return events
 
     def shares(c):
@@ -250,9 +267,9 @@
         hid[:, cut] = act.astype(hid.dtype)
 
     def expert_out(c, p):
-        @pl.loop(0, half // wtile)
+        @pl.loop(0, piece // wtile)
         def _(n):
-            cut = pl.ds(pl.multiple_of(p * half + n * wtile, wtile), wtile)
+            cut = pl.ds(pl.multiple_of(p * piece + n * wtile, wtile), wtile)
             done = jnp.dot(hid[...], wd[:, cut], preferred_element_type=jnp.float32)
             part[c, :, cut] = done.astype(part.dtype)
 
@@ -260,21 +277,25 @@
         events = []
         for n in range(hidden // htile):
             events.append(functools.partial(expert_in, c, n))
-        for p in range(2):
+        for p in every:
             events.append(lambda p=p: (expert_out(c, p), scatter_first(c, p)))
         return events
 
     def scatter_first(c, p):
         a, b = coords[p][0], coords[p][1]
-        for aa in (1 - a, a):
-            for zz in range(chain):
-                src = part.at[c, span(slot(p, zz, aa, 1 - b)), scols[p]]
-                k = zz * 2 + aa
-                send("s", src, rb.at[c, p, k], srecv.at[c, p, k],
-                     {"expert": slot(p, z, a, 1 - b)})
-
-    def scatter_second(c, p, zz):
-        a, b = coords[p][0], coords[p][1]
+        far = [(z + chain - 1 - i) % chain for i in range(chain)]
+        dests = [(zz, aa) for aa in (1 - a, a) for zz in far]
+        if p in early:
+            dests = [(zz, aa) for zz in far for aa in (1 - a, a)]
+        for zz, aa in dests:
+            src = part.at[c, span(slot(p, zz, aa, 1 - b)), scols[p]]
+            k = zz * 2 + aa
+            send("s", src, rb.at[c, p, k], srecv.at[c, p, k],
+                 {"expert": slot(p, z, a, 1 - b)})
+
+    def scatter_second(c, p, i):
+        a, b = coords[p][0], coords[p][1]
+        zz = (z + chain - 1 - i) % chain
         k = zz * 2 + 1 - a
         arrived(rb.at[c, p, k], srecv.at[c, p, k])
         here = (c, span(slot(p, zz, 1 - a, b)), scols[p])
@@ -283,64 +304,86 @@
         send("s", part.at[here], ra.at[c, p, zz], srecv.at[c, p, 2 * chain + zz],
              {"expert": slot(p, z, 1 - a, b)})
 
-    def summed(c, p, zz):
-        a, b = coords[p][0], coords[p][1]
-        k = zz * 2 + a
+    def summed(c, p, zz, aa):
+        b = coords[p][1]
+        k = zz * 2 + aa
         arrived(rb.at[c, p, k], srecv.at[c, p, k])
-        arrived(ra.at[c, p, zz], srecv.at[c, p, 2 * chain + zz])
-        own = part[c, span(slot(p, zz, a, b)), scols[p]].astype(jnp.float32)
-        return own + rb[c, p, k].astype(jnp.float32) + ra[c, p, zz].astype(jnp.float32)
-
-    def passing(c, p, way, zz):
-        k = (3 + way) * chain + zz
-        arrived(rz.at[c, p, way, zz], srecv.at[c, p, k])
-        return rz[c, p, way, zz].astype(jnp.float32)
-
-    def scatter_side(c, p, way, zz, cond, behind, target):
-        a, b = coords[p][0], coords[p][1]
-        here = (c, span(slot(p, zz, a, b)), scols[p])
-
-        @pl.when(cond)
+        own = part[c, span(slot(p, zz, aa, b)), scols[p]].astype(jnp.float32)
+        total = own + rb[c, p, k].astype(jnp.float32)
+        if p in late:
+            arrived(ra.at[c, p, zz], srecv.at[c, p, 2 * chain + zz])
+            total += ra[c, p, zz].astype(jnp.float32)
+        return total
+
+    def passing(c, p, way, zz, aa):
+        k = (zz * 2 + aa) * 2 + way
+        arrived(rz.at[c, p, k], srecv.at[c, p, 3 * chain + k])
+        return rz[c, p, k].astype(jnp.float32)
+
+    def scatter_side(c, p, way, zz, aa, cond, behind, target):
+        here = (c, span(slot(p, zz, aa, coords[p][1])), scols[p])
+        k = (zz * 2 + aa) * 2 + way
+
+        @pl.when(jnp.logical_and(cond, jnp.logical_not(behind)))
         def _():
-            part[here] = summed(c, p, zz).astype(part.dtype)
+            part[here] = summed(c, p, zz, aa).astype(part.dtype)
 
         @pl.when(jnp.logical_and(cond, behind))
         def _():
-            more_of = part[here].astype(jnp.float32) + passing(c, p, way, zz)
-            part[here] = more_of.astype(part.dtype)
-
-        send("s", part.at[here], rz.at[c, p, way, zz],
-             srecv.at[c, p, (3 + way) * chain + zz], {"expert": target}, cond)
+            total = summed(c, p, zz, aa) + passing(c, p, way, zz, aa)
+            part[here] = total.astype(part.dtype)
+
+        send("s", part.at[here], rz.at[c, p, k], srecv.at[c, p, 3 * chain + k],
+             {"expert": target}, cond)
 
     def scatter_chain(c, p, s):
-        scatter_side(c, p, 0, z + s, z + s < chain, less, me + 4)
-        scatter_side(c, p, 1, z - s, z - s >= 0, more, me - 4)
+        a = coords[p][0]
+        for aa in (1 - a, a) if p in early else (a,):
+            scatter_side(c, p, 0, z + s, aa, z + s < chain, less, me + 4)
+            scatter_side(c, p, 1, z - s, aa, z - s >= 0, more, me - 4)
+
+    def landed(c, p, aa):
+        fin[:, :] = summed(c, p, z, aa)
+
+        @pl.when(less)
+        def _():
+            fin[:, :] += passing(c, p, 0, z, aa)
+
+        @pl.when(more)
+        def _():
+            fin[:, :] += passing(c, p, 1, z, aa)
+
+    def scatter_turn(c, p):
+        a, b = coords[p][0], coords[p][1]
+        landed(c, p, 1 - a)
+        here = (c, span(slot(p, z, 1 - a, b)), scols[p])
+        part[here] = fin[:, :].astype(part.dtype)
+        send("s", part.at[here], ra.at[c, p, 0], srecv.at[c, p, 2 * chain],
+             {"expert": slot(p, z, 1 - a, b)})
 
     def scatter_last(c, p):
         lines = pl.ds(c * take, take)
-        total = summed(c, p, z)
+        landed(c, p, coords[p][0])
         stream = res_ref[lines, scols[p]].astype(jnp.float32) + att_ref[
             lines, scols[p]
         ].astype(jnp.float32)
-        fin[:, :] = total
-
-        @pl.when(less)
-        def _():
-            fin[:, :] += passing(c, p, 0, z)
-
-        @pl.when(more)
-        def _():
-            fin[:, :] += passing(c, p, 1, z)
-
-        o_ref[lines, scols[p]] = (stream + fin[:, :]).astype(o_ref.dtype)
+        total = stream + fin[:, :]
+        if p in early:
+            arrived(ra.at[c, p, 0], srecv.at[c, p, 2 * chain])
+            total += ra[c, p, 0].astype(jnp.float32)
+        o_ref[lines, scols[p]] = total.astype(o_ref.dtype)
 
     def scatter_events(c):
-        def both(f, *rest):
-            return lambda: [f(c, p, *rest) for p in range(2)]
-
-        events = [both(scatter_second, zz) for zz in range(chain)]
-        events += [both(scatter_chain, s) for s in range(chain - 1, 0, -1)]
-        events.append(both(scatter_last))
+        events = []
+        for s in range(chain - 1, 0, -1):
+            events.append(over(early, scatter_chain, c, s))
+            events.append(over(late, scatter_second, c, chain - 1 - s))
+        events.append(over(late, scatter_second, c, chain - 1))
+        events.append(over(early, scatter_turn, c))
+        for s in range(chain - 1, 0, -1):
+            events.append(over(late, scatter_chain, c, s))
+        events.append(over(late, scatter_last, c))
+        events.append(over(early, scatter_last, c))
         return events
 
     def merged(first, second):
@@ -355,7 +398,7 @@
     order = fetch[0][:1] + [start_weights] + fetch[0][1:3] + fetch[1][:1] + fetch[0][3:]
     order += [lambda: [wait_weights(i) for i in range(3)]]
     order += merged(fetch[1][1:], work[0])
-    order += merged(work[1], back[0]) + back[1]
+    order += merged(work[1], back[0][:7]) + merged(back[0][7:], back[1][:7]) + back[1][7:]
     for event in order:
         event()
     for cond, end in pending:
@@ -381,8 +424,8 @@
     extra = jnp.pad(extra, ((0, 0), (0, lanes - 2 * experts)))
     packed = jnp.concatenate([normed, extra], axis=1)
     bf16 = jnp.bfloat16
-    copies = 2 * CHUNKS * (4 + 6 * (chain - 1) + 1 + 2 * (chain - 1))
-    sums = 2 * CHUNKS * (3 * chain + 2 * (chain - 1))
+    copies = PARTS * CHUNKS * (7 + 8 * (chain - 1))
+    sums = PARTS * CHUNKS * (1 + 3 * chain + 4 * (chain - 1))
     vmem, anywhere = pl.BlockSpec(memory_space=pltpu.VMEM), pl.BlockSpec(memory_space=pl.ANY)
     return pl.pallas_call(
         functools.partial(fused_kernel, experts),
@@ -396,15 +439,15 @@
             pltpu.VMEM((width, hidden), bf16),
             pltpu.VMEM((hidden, width), bf16),
             pltpu.VMEM((experts * take, hidden), bf16),
-            pltpu.VMEM((CHUNKS, 2, 2 * chain, take, width // 2), bf16),
-            pltpu.VMEM((CHUNKS, 2, chain, take, width // 2), bf16),
-            pltpu.VMEM((CHUNKS, 2, 2, chain, take, width // 2), bf16),
-            pltpu.VMEM((take, width // 2), jnp.float32),
+            pltpu.VMEM((CHUNKS, PARTS, 2 * chain, take, width // PARTS), bf16),
+            pltpu.VMEM((CHUNKS, PARTS, chain, take, width // PARTS), bf16),
+            pltpu.VMEM((CHUNKS, PARTS, 4 * chain, take, width // PARTS), bf16),
+            pltpu.VMEM((take, width // PARTS), jnp.float32),
             pltpu.SemaphoreType.DMA((10,)),
             pltpu.SemaphoreType.DMA((copies,)),
-            pltpu.SemaphoreType.DMA((CHUNKS, 2, experts)),
+            pltpu.SemaphoreType.DMA((CHUNKS, PARTS, experts)),
             pltpu.SemaphoreType.DMA((sums,)),
-            pltpu.SemaphoreType.DMA((CHUNKS, 2, 5 * chain)),
+            pltpu.SemaphoreType.DMA((CHUNKS, PARTS, 7 * chain)),
         ],
         compiler_params=pltpu.CompilerParams(
             collective_id=0, has_side_effects=True, vmem_limit_bytes=66 * 1000 * 1000

time: 187 us -> 178 us (0.952)
  Pallas kernels: 180 us -> 171 us
    pallas_call x1, Pallas kernels: 180 us -> 171 us  [multicast_shards(): pl.pallas_call(functools.partial(fused_kernel, experts), out_shape=jax.Sh...]
where the time goes in v3:
time: 178 us; the launch traced here: 177 us
  Pallas kernels  171 us (96%)
  other arithmetic  4.54 us (3%)
  local copies, waits for them, and re-layouts  2.03 us (1%)
    pallas_call x1, Pallas kernels, multicast_shards(): pl.pallas_call(functools.partial(fused_kernel, experts), out_shape=jax.Sh...  171 us

profile of v3, /device:TPU:0, one launch (start us, length us, event | category | flops | bytes accessed | tf_op | source)
XLA Modules:
  0.0 177.4 jit_solution(17693779548672557308)
XLA Ops:
  0.0 1.5 multiply_reduce_fusion
  1.5 0.7 select_reduce_fusion
  2.2 0.1 copy.14
  2.3 0.1 copy.13
  2.4 0.1 fusion.2
  2.5 1.4 multiply_convert_fusion
  3.9 0.8 pad_maximum_fusion.x_ref
  4.7 170.8 %shard_map.82 = bf16[64,4096]{1,0:T(8,128)(2,1)} custom-call(bf16[64,4224]{1,0:T(8,128)(2,1)} %pad_maximum_fusion.x_ref, bf16[64,4096]{1,0:T(8,128)(2,1)} %res_ref.1, bf16[64,4096]{1,0:T(8,128)(2,1)} %att_ref.1, bf16[4096,384]{1,0:T(8,128)(2,1)} %bitcast.3, bf16[4096,384]{1,0:T(8,128)(2,1)} %bitcast.4, bf16[384,4096]{1,0:T(8,128)(2,1)} %bitcast.5), custom_call_target="tpu_custom_call" | custom-call | tf_op jit(solution)/shard_map/pallas_call | solution.py:430
  175.6 1.9 %copy.17 = bf16[64,4096]{1,0:T(8,128)(2,1)} copy(bf16[64,4096]{1,0:T(8,128)(2,1)} %shard_map.82) | data formatting | bytes 1048576
  (3 shorter events, 0.0 us)

commit v4 on v3

--- a/solution.py
+++ b/solution.py
@@ -398,7 +398,8 @@
     order = fetch[0][:1] + [start_weights] + fetch[0][1:3] + fetch[1][:1] + fetch[0][3:]
     order += [lambda: [wait_weights(i) for i in range(3)]]
     order += merged(fetch[1][1:], work[0])
-    order += merged(work[1], back[0][:7]) + merged(back[0][7:], back[1][:7]) + back[1][7:]
+    ahead = back[0][0:6:2] + back[0][1:6:2] + back[0][6:7]
+    order += merged(work[1], ahead) + merged(back[0][7:], back[1][:7]) + back[1][7:]
     for event in order:
         event()
     for cond, end in pending:

time: 178 us -> 178 us (level)
  no operation moved by 1% of the time
where the time goes in v4:
time: 178 us
  Pallas kernels  171 us (96%)
  other arithmetic  4.54 us (3%)
  local copies, waits for them, and re-layouts  2.03 us (1%)
    pallas_call x1, Pallas kernels, multicast_shards(): pl.pallas_call(functools.partial(fused_kernel, experts), out_shape=jax.Sh...  171 us

profile of v4, /device:TPU:0, one launch (start us, length us, event | category | flops | bytes accessed | tf_op | source)
XLA Modules:
  0.0 177.9 jit_solution(7505980540975693500)
XLA Ops:
  0.0 1.5 multiply_reduce_fusion
  1.5 0.7 select_reduce_fusion
  2.2 0.1 copy.14
  2.3 0.1 copy.13
  2.4 0.1 fusion.2
  2.5 1.4 multiply_convert_fusion
  3.9 0.8 pad_maximum_fusion.x_ref
  4.7 171.3 %shard_map.82 = bf16[64,4096]{1,0:T(8,128)(2,1)} custom-call(bf16[64,4224]{1,0:T(8,128)(2,1)} %pad_maximum_fusion.x_ref, bf16[64,4096]{1,0:T(8,128)(2,1)} %res_ref.1, bf16[64,4096]{1,0:T(8,128)(2,1)} %att_ref.1, bf16[4096,384]{1,0:T(8,128)(2,1)} %bitcast.3, bf16[4096,384]{1,0:T(8,128)(2,1)} %bitcast.4, bf16[384,4096]{1,0:T(8,128)(2,1)} %bitcast.5), custom_call_target="tpu_custom_call" | custom-call | tf_op jit(solution)/shard_map/pallas_call | solution.py:431
  176.1 1.9 %copy.17 = bf16[64,4096]{1,0:T(8,128)(2,1)} copy(bf16[64,4096]{1,0:T(8,128)(2,1)} %shard_map.82) | data formatting | bytes 1048576
  (3 shorter events, 0.0 us)
